TPU v7x, 32 devices: a whole 2x2x4 slice. The times are simulated.
32 devices in a mesh: dp: 4 (over x, core), ctx: 2 (over y), head: 4 (over z).
Axes of the slice: x: 2, y: 2, z: 4, core: 2. Of those that a mesh axis runs over, the one named last changes fastest.
Arguments:
- inputs: bfloat16 [16, 256, 1024], P('dp', 'ctx', 'head'), parts along dimension 0, may hold values from -6 to 6
- lengths: int32 [16], P('dp'), parts along dimension 0, may hold values from 1 to 640, 1024 in all
- proj_in: bfloat16 [1024, 4, 1024], P(None, None, 'head'), may hold values from -0.1875 to 0.1875
- proj_out: bfloat16 [1024, 1024], P('head'), may hold values from -0.1875 to 0.1875
Outputs:
- layer_out: bfloat16 [8, 2, 256, 1024], P(('dp', 'ctx'), None, None, 'head'), parts along dimension 0
There are 4 independent parts, one for each index of `dp`. A program takes and returns all parts, laid end to end along the dimension named above; an argument that names none is the same for every part. Nothing has to cross between parts.
Inputs may be any that keep to these rules, and one draw needn't show every extreme that they name: The 4 histories lie end to end in the packed rows; the lengths sum to 1024 and the longest is exactly 640.
All inputs are finite; a program needn't handle non-finite values.
Results may differ from a plain program's by a relative error of at most 0.0055.
Values may be sent and summed in bfloat16 or wider, within the bound.
No kernel may reach another device: no remote copies, remote signals or barrier semaphores. Data moves between devices by JAX's collectives and lax.ppermute only.
A program may use at most 64 MiB of HBM per device.

v0:
```python
import math
import jax
import jax.numpy as jnp
from jax import lax
from jax.sharding import PartitionSpec as P

HDIM = 128


def layer_norm(values, epsilon):
    center = values - jnp.mean(values, axis=-1, keepdims=True)
    spread = jnp.mean(center * center, axis=-1, keepdims=True)
    return center * lax.rsqrt(spread + epsilon)


def silu_round(values):
    return jax.nn.silu(values).astype(jnp.bfloat16)


def body(inputs, lengths, proj_in, proj_out):
    context_size = lax.axis_size("ctx")
    own_index = lax.axis_index("ctx")
    block_total, stripe, width_part = inputs.shape
    block_len = stripe * context_size
    row_count = 2 * block_len
    heads_dev = proj_in.shape[2] // HDIM
    reordered = jnp.stack([inputs[:context_size], inputs[context_size:][::-1]], axis=1)
    reordered = reordered.reshape(block_total, stripe, width_part)
    own_rows = lax.all_to_all(reordered, "ctx", split_axis=0, concat_axis=1, tiled=True)
    full_rows = lax.all_gather(own_rows, "head", axis=2, tiled=True)
    normed = layer_norm(full_rows.reshape(row_count, -1).astype(jnp.float32), 1e-06).astype(
        jnp.bfloat16
    )
    user_ends = jnp.cumsum(lengths)

    def segment(position):
        return jnp.sum((position[:, None] >= user_ends[None, :]).astype(jnp.int32), axis=1)

    offsets = jnp.arange(block_len, dtype=jnp.int32)
    own_blocks = jnp.stack([own_index, 2 * context_size - 1 - own_index])
    query_pos = (own_blocks[:, None] * block_len + offsets[None, :]).reshape(-1)
    query_seg = segment(query_pos)
    score_scale = 1.0 / math.sqrt(HDIM)
    projected = silu_round(
        jnp.einsum("rd,dgc->rgc", normed, proj_in, preferred_element_type=jnp.float32)
    )
    gating = projected[:, 0]
    queries = projected[:, 2]
    key_pair = (
        projected[:, 3].reshape(2, block_len, -1),
        projected[:, 1].reshape(2, block_len, -1),
    )

    def loader(shards, lead_row, tile_rows):
        key_rows = lax.dynamic_slice_in_dim(shards[0], lead_row, tile_rows, 0)
        value_rows = lax.dynamic_slice_in_dim(shards[1], lead_row, tile_rows, 0)
        return (
            key_rows.reshape(tile_rows * block_len, heads_dev, HDIM),
            value_rows.reshape(tile_rows * block_len, heads_dev, HDIM),
        )

    query_heads = queries.reshape(row_count, heads_dev, HDIM)
    zero_acc = jnp.zeros((row_count, heads_dev, HDIM), jnp.float32)
    shards = (
        lax.all_gather(key_pair[0], "ctx", axis=0, tiled=True),
        lax.all_gather(key_pair[1], "ctx", axis=0, tiled=True),
    )
    piece_rows = shards[0].shape[0]
    tile_rows = 4

    def one_tile(tile_index, partial_value):
        lead_row = tile_index * tile_rows
        listed = lead_row + jnp.arange(tile_rows, dtype=jnp.int32)
        holder = listed // 2
        block_ids = jnp.where(listed % 2 == 0, holder, 2 * context_size - 1 - holder)
        key_pos = (block_ids[:, None] * block_len + offsets[None, :]).reshape(-1)
        allowed = (query_seg[:, None] == segment(key_pos)[None, :]) & (
            key_pos[None, :] <= query_pos[:, None]
        )
        key_rows, value_rows = loader(shards, lead_row, tile_rows)
        scores = (
            jnp.einsum("qhd,khd->hqk", query_heads, key_rows, preferred_element_type=jnp.float32)
            * score_scale
        )
        weights = jnp.where(allowed[None], jax.nn.silu(scores), 0.0).astype(jnp.bfloat16)
        return partial_value + jnp.einsum(
            "hqk,khd->qhd", weights, value_rows, preferred_element_type=jnp.float32
        )

    attended = lax.fori_loop(0, piece_rows // tile_rows, one_tile, zero_acc)
    gate_prod = layer_norm(attended, 1e-05) * gating.reshape(row_count, heads_dev, HDIM).astype(
        jnp.float32
    )
    gate_prod = gate_prod.astype(jnp.bfloat16).reshape(row_count, -1)
    columns = lax.all_to_all(proj_out, "head", split_axis=1, concat_axis=0, tiled=True)
    summed = jnp.dot(
        lax.all_gather(gate_prod, "head", axis=1, tiled=True),
        columns,
        preferred_element_type=jnp.float32,
    )
    result = (own_rows.reshape(row_count, -1).astype(jnp.float32) + summed).astype(jnp.bfloat16)
    return result.reshape(1, 2, block_len, -1)


def solution(mesh):
    return jax.shard_map(
        body,
        mesh=mesh,
        in_specs=(P("dp", "ctx", "head"), P("dp"), P(None, None, "head"), P("head", None)),
        out_specs=P(("dp", "ctx"), None, None, "head"),
        check_vma=False,
    )
```

profile of v0, /device:TPU:0, one launch (start us, length us, event | category | flops | bytes accessed | tf_op | source)
XLA Modules:
  0.0 122.5 jit_solution(3696694843933152079)
XLA Ops:
  6.5 0.0 copy-start
  6.5 0.0 copy-start.2
  6.5 0.0 all-gather.3.cloned.1.call-start
  6.5 1.1 slice_bitcast_fusion
  7.7 9.2 %all_to_all.37 = bf16[4,128,256]{2,1,0:T(8,128)(2,1)S(1)} all-to-all(bf16[4,128,256]{2,1,0:T(8,128)(2,1)S(1)} %bitcast.59), channel_id=1, replica_groups=mesh['dp'=4,'ctx'=2,'head'=4] {'ctx'}, dimensions={0} | all-to-all | bytes 524288 | tf_op jit(solution)/shard_map/all_to_all | solution.py:29
  17.0 0.7 copy.34
  17.7 0.0 all-gather.3.cloned.1.call-update
  17.7 0.0 all-gather.5.cloned.1.call-start
  17.8 0.1 add_multiply_fusion
  17.9 0.1 add_bitcast_fusion.1
  17.9 0.1 add_bitcast_fusion
  18.0 0.0 copy-done.2
  18.0 0.2 reduce-window.8
  18.2 0.1 convert_reduce_fusion.2
  18.3 0.1 convert_reduce_fusion.1
  18.4 1.3 %compare_and_fusion = pred[512,1024]{1,0:T(8,128)(4,1)} fusion(s32[1024]{0:T(1024)S(1)} %bitcast.63, s32[1024]{0:T(1024)S(1)} %convert_reduce_fusion.1, s32[512]{0:T(512)S(1)} %bitcast.65, s32[512]{0:T(512)S(1)} %convert_reduce_fusion.2), kind=kLoop, calls=%fused_computation.8 | loop fusion | flops 1572864 | bytes 536576 | tf_op jit(solution)/shard_map/while/body/eval_jaxpr/and | solution.py:77
  19.7 28.5 %all-gather.3.cloned.1.call-done = bf16[2,256,1024]{2,1,0:T(8,128)(2,1)} async-done(((bf16[2,256,256]{2,1,0:T(8,128)(2,1)}), bf16[2,256,1024]{2,1,0:T(8,128)(2,1)}) %all-gather.3.cloned.1.call-update) | async-done | bytes 1048592 | tf_op jit(solution)/shard_map/all_gather | solution.py:30
  48.2 0.0 copy-start.1
  48.2 1.5 %convert_reduce_fusion = f32[2,256]{1,0:T(2,128)S(1)} fusion(bf16[2,256,1024]{2,1,0:T(8,128)(2,1)} %all-gather.3.cloned.1.call-done), kind=kLoop, calls=%fused_computation.14 | loop fusion | flops 1048064 | bytes 1050624 | tf_op jit(solution)/shard_map/reduce_sum | solution.py:11
  49.7 1.6 %multiply_reduce_fusion = f32[2,256]{1,0:T(2,128)S(1)} fusion(bf16[2,256,1024]{2,1,0:T(8,128)(2,1)} %all-gather.3.cloned.1.call-done, f32[2,256]{1,0:T(2,128)S(1)} %get-tuple-element.40), kind=kLoop, calls=%fused_computation.7 | loop fusion | flops 2096640 | bytes 1052672 | tf_op jit(solution)/shard_map/reduce_sum | solution.py:12
  51.4 0.0 copy-done.1
  51.4 0.3 fusion.1
  51.7 0.0 copy-done
  51.7 1.5 %multiply_convert_fusion = bf16[512,4,256]{2,0,1:T(8,128)(2,1)S(1)} fusion(bf16[1024,4,256]{2,1,0:T(4,128)(2,1)S(1)} %copy-done, bf16[512,1024]{1,0:T(8,128)(2,1)S(1)} %fusion.1), kind=kOutput, calls=%fused_computation.6 | convolution fusion | flops 1076363264 | bytes 4194304 | tf_op jit(solution)/shard_map/rd,dgc->rgc/dot_general | solution.py:45
  53.2 0.9 fusion.22
  54.1 7.7 %all_gather.14 = bf16[4,256,256]{2,1,0:T(8,128)(2,1)S(1)} all-gather(bf16[2,256,256]{2,1,0:T(8,128)(2,1)S(1)} %bitcast.56), channel_id=1, replica_groups=mesh['dp'=4,'ctx'=2,'head'=4] {'ctx'}, dimensions={0}, use_global_device_ids=true | all-gather | bytes 786432 | tf_op jit(solution)/shard_map/all_gather | solution.py:65
  61.8 0.9 reshape.244
  62.7 7.9 %all_gather.13 = bf16[4,256,256]{2,1,0:T(8,128)(2,1)S(1)} all-gather(bf16[2,256,256]{2,1,0:T(8,128)(2,1)S(1)} %bitcast.55), channel_id=1, replica_groups=mesh['dp'=4,'ctx'=2,'head'=4] {'ctx'}, dimensions={0}, use_global_device_ids=true | all-gather | bytes 786432 | tf_op jit(solution)/shard_map/all_gather | solution.py:66
  70.6 0.9 reshape.251
  71.5 0.1 reshape_squeeze.11
  71.6 3.5 %fusion.23 = (f32[512,2]{0,1:T(2,128)S(1)}, f32[512,2,128]{0,2,1:T(8,128)S(1)}) fusion(pred[512,1024]{1,0:T(8,128)(4,1)} %compare_and_fusion, bf16[1024,2,128]{2,1,0:T(2,128)(2,1)} %reshape.244, bf16[512,2,128]{2,1,0:T(2,128)(2,1)S(1)} %reshape_squeeze.11, bf16[1024,2,128]{2,1,0:T(2,128)(2,1)} %reshape.251), kind=kOutput, calls=%fused_computation.45 | convolution fusion | flops 544340992 | bytes 2363392 | tf_op jit(solution)/shard_map/while/body/eval_jaxpr/hqk,khd->qhd/dot_general | solution.py:86
  75.1 0.1 multiply_reduce_fusion.1
  75.2 1.2 %copy.43 = f32[512,1,256]{0,2,1:T(8,128)S(1)} copy(f32[512,1,256]{2,0,1:T(8,128)} %get-tuple-element.24) | data formatting | bytes 1048576 | tf_op jit(solution)/shard_map/convert_element_type | solution.py:91
  76.5 0.8 multiply_convert_fusion.1
  77.3 0.0 all-gather.5.cloned.1.call-update
  77.3 2.1 %copy.40 = bf16[256,1024]{0,1:T(8,128)(2,1)} copy(bf16[256,1024]{1,0:T(8,128)(2,1)} %param.7) | data formatting | bytes 1048576 | tf_op args[3]
  79.4 3.5 %all-to-all-start.1 = ((bf16[256,4,256]{0,2,1:T(8,128)(2,1)}), bf16[256,4,256]{0,2,1:T(8,128)(2,1)S(1)}, u32[]{:S(2)}, u32[]{:S(2)}) async-start(bf16[256,4,256]{0,2,1:T(8,128)(2,1)} %bitcast.19), calls=%async_computation.1 | async-start | bytes 1048576 | tf_op jit(solution)/shard_map/all_to_all | solution.py:95
  82.9 25.4 %all-to-all-done.1 = bf16[256,4,256]{0,2,1:T(8,128)(2,1)S(1)} async-done(((bf16[256,4,256]{0,2,1:T(8,128)(2,1)}), bf16[256,4,256]{0,2,1:T(8,128)(2,1)S(1)}, u32[]{:S(2)}, u32[]{:S(2)}) %all-to-all-start.1) | async-done | bytes 524320 | tf_op jit(solution)/shard_map/all_to_all | solution.py:95
  108.4 1.0 copy.41
  109.4 3.7 %all-gather.5.cloned.1.call-done = bf16[512,1024]{0,1:T(8,128)(2,1)} async-done(((bf16[512,256]{0,1:T(8,128)(2,1)}), bf16[512,1024]{0,1:T(8,128)(2,1)}) %all-gather.5.cloned.1.call-update) | async-done | bytes 1048592 | tf_op jit(solution)/shard_map/all_gather | solution.py:97
  113.1 2.5 %fusion.6 = bf16[512,256]{1,0:T(8,128)(2,1)} fusion(f32[512,256]{1,0:T(8,128)S(1)} %bitcast.60, bf16[512,1024]{0,1:T(8,128)(2,1)} %all-gather.5.cloned.1.call-done, bf16[1024,256]{1,0:T(8,128)(2,1)} %bitcast.61), kind=kOutput, calls=%fused_computation.12 | convolution fusion | flops 268697600 | bytes 2359296 | tf_op jit(solution)/shard_map/dot_general | solution.py:96
  (12 shorter events, 0.1 us)
Async XLA Ops:
  6.5 45.2 %copy-start = (bf16[1024,4,256]{2,1,0:T(4,128)(2,1)S(1)}, bf16[1024,4,256]{2,1,0:T(4,128)(2,1)}, u32[]{:S(2)}) copy-start(bf16[1024,4,256]{2,1,0:T(4,128)(2,1)} %param.6) | copy-start | bytes 6291460
  6.5 11.5 %copy-start.2 = (s32[4]{0:T(128)S(1)}, s32[4]{0:T(128)}, u32[]{:S(2)}) copy-start(s32[4]{0:T(128)} %param.5) | copy-start | bytes 52
  6.5 41.6 %all-gather.3.cloned.1.call-start = ((), (), s32[]{:S(2)}) async-start(), calls=%async_computation.2 | async-start | bytes 1310720 | tf_op jit(solution)/shard_map/all_gather | solution.py:30
  17.7 95.4 %all-gather.5.cloned.1.call-start = ((), (), s32[]{:S(2)}) async-start(), calls=%async_computation.3 | async-start | bytes 1310720 | tf_op jit(solution)/shard_map/all_gather | solution.py:97
  48.2 3.2 %copy-start.1 = (bf16[2,256,1024]{2,1,0:T(8,128)(2,1)S(1)}, bf16[2,256,1024]{2,1,0:T(8,128)(2,1)}, u32[]{:S(2)}) copy-start(bf16[2,256,1024]{2,1,0:T(8,128)(2,1)} %all-gather.3.cloned.1.call-done) | copy-start | bytes 3145732
  79.4 29.0 %all-to-all-start.1 = ((bf16[256,4,256]{0,2,1:T(8,128)(2,1)}), bf16[256,4,256]{0,2,1:T(8,128)(2,1)S(1)}, u32[]{:S(2)}, u32[]{:S(2)}) async-start(bf16[256,4,256]{0,2,1:T(8,128)(2,1)} %bitcast.19), calls=%async_computation.1 | async-start | bytes 1048576 | tf_op jit(solution)/shard_map/all_to_all | solution.py:95
Sparse Core Ops, SparseCore 0:
  17.8 30.2 all-gather.2
  77.4 35.6 all-gather.4
where the time goes:
time: 123 us; the launch traced here: 122 us
  waiting for transfers between devices  57.7 us (47%)
  blocking collectives  24.8 us (20%)
  between operations  13.5 us (11%)
  local copies, waits for them, and re-layouts  8.2 us (7%)
  matrix products  7.57 us (6%)
  other arithmetic  7.19 us (6%)
  starting transfers between devices  3.51 us (3%)
    all_gather x1, waiting for transfers between devices, body(): full_rows = lax.all_gather(own_rows, 'head', axis=2, tiled=True)  28.5 us
    all_to_all x1, waiting for transfers between devices, body(): lax.all_to_all(proj_out, 'head', split_axis=1, concat_axis=0, tiled=True)  25.4 us
    all_to_all x1, blocking collectives, body(): lax.all_to_all(reordered, 'ctx', split_axis=0, concat_axis=1, tiled=True)  9.24 us
    all_gather x1, blocking collectives, body(): lax.all_gather(key_pair[1], 'ctx', axis=0, tiled=True)  7.86 us
    all_gather x1, blocking collectives, body(): lax.all_gather(key_pair[0], 'ctx', axis=0, tiled=True)  7.68 us
    all_gather x1, waiting for transfers between devices, body(): lax.all_gather(gate_prod, 'head', axis=1, tiled=True)  3.71 us
    dot_general x1, matrix products, one_tile(): jnp.einsum('hqk,khd->qhd', weights, value_rows, preferred_element_type=jn...  3.53 us
    all_to_all x1, starting transfers between devices, body(): lax.all_to_all(proj_out, 'head', split_axis=1, concat_axis=0, tiled=True)  3.47 us
  transfers between devices with their start and end apart: 3, of which 3 were waited for; matrix products, arithmetic and copies ran while one was open for 4% of the time, Pallas kernels for 0%

commit v1 on v0

--- a/solution.py
+++ b/solution.py
@@ -27,7 +27,12 @@
     reordered = jnp.stack([inputs[:context_size], inputs[context_size:][::-1]], axis=1)
     reordered = reordered.reshape(block_total, stripe, width_part)
     own_rows = lax.all_to_all(reordered, "ctx", split_axis=0, concat_axis=1, tiled=True)
-    full_rows = lax.all_gather(own_rows, "head", axis=2, tiled=True)
+    ring = [own_rows]
+    for hop in range(3):
+        ring.append(lax.ppermute(ring[-1], "head", [(dev, (dev + 1) % 4) for dev in range(4)]))
+    full_rows = jnp.roll(
+        jnp.concatenate(ring[::-1], axis=2), (lax.axis_index("head") + 1) * ring[0].shape[2], axis=2
+    )
     normed = layer_norm(full_rows.reshape(row_count, -1).astype(jnp.float32), 1e-06).astype(
         jnp.bfloat16
     )

time: 123 us -> 112 us (0.911)
  blocking collectives: 24.8 us -> 14.6 us
  starting transfers between devices: 3.51 us -> 9.6 us
  waiting for transfers between devices: 57.7 us -> 53.2 us
  other arithmetic: 7.19 us -> 5.35 us
    all_gather x1 -> x0, waiting for transfers between devices: 28.5 us -> none  [body(): full_rows = lax.all_gather(own_rows, 'head', axis=2, tiled=True)]
    ppermute x0 -> x3, waiting for transfers between devices: none -> 22.2 us  [body(): lax.ppermute(ring[-1], 'head', [(dev, (dev + 1) % 4) for dev in range(4)])]
    all_to_all x1 -> x0, blocking collectives: 9.24 us -> none  [body(): lax.all_to_all(reordered, 'ctx', split_axis=0, concat_axis=1, tiled=True)]
    all_to_all x0 -> x1, waiting for transfers between devices: none -> 5.79 us  [body(): lax.all_to_all(reordered, 'ctx', split_axis=0, concat_axis=1, tiled=True)]
    all_to_all x0 -> x1, starting transfers between devices: none -> 4.26 us  [body(): lax.all_to_all(reordered, 'ctx', split_axis=0, concat_axis=1, tiled=True)]
    all_to_all x1, waiting for transfers between devices: 25.4 us -> 23 us  [body(): lax.all_to_all(proj_out, 'head', split_axis=1, concat_axis=0, tiled=True)]
    ppermute x0 -> x3, starting transfers between devices: none -> 1.85 us  [body(): lax.ppermute(ring[-1], 'head', [(dev, (dev + 1) % 4) for dev in range(4)])]
    all_gather x1, waiting for transfers between devices: 3.71 us -> 2.11 us  [body(): lax.all_gather(gate_prod, 'head', axis=1, tiled=True)]
  transfers between devices with their start and end apart: 3 -> 6, of which waited for: 3 -> 6; matrix products, arithmetic and copies ran while one was open for 4% -> 4% of each run, Pallas kernels for 0% -> 0%
where the time goes in v1:
time: 112 us
  waiting for transfers between devices  53.2 us (48%)
  blocking collectives  14.6 us (13%)
  between operations  13.6 us (12%)
  starting transfers between devices  9.6 us (9%)
  local copies, waits for them, and re-layouts  7.74 us (7%)
  matrix products  7.58 us (7%)
  other arithmetic  5.35 us (5%)
    all_to_all x1, waiting for transfers between devices, body(): lax.all_to_all(proj_out, 'head', split_axis=1, concat_axis=0, tiled=True)  23 us
    ppermute x3, waiting for transfers between devices, body(): lax.ppermute(ring[-1], 'head', [(dev, (dev + 1) % 4) for dev in range(4)])  22.2 us
    all_gather x1, blocking collectives, body(): lax.all_gather(key_pair[0], 'ctx', axis=0, tiled=True)  7.59 us
    all_gather x1, blocking collectives, body(): lax.all_gather(key_pair[1], 'ctx', axis=0, tiled=True)  7.03 us
    all_to_all x1, waiting for transfers between devices, body(): lax.all_to_all(reordered, 'ctx', split_axis=0, concat_axis=1, tiled=True)  5.79 us
    all_to_all x1, starting transfers between devices, body(): lax.all_to_all(reordered, 'ctx', split_axis=0, concat_axis=1, tiled=True)  4.26 us
    dot_general x1, matrix products, one_tile(): jnp.einsum('hqk,khd->qhd', weights, value_rows, preferred_element_type=jn...  3.53 us
    all_to_all x1, starting transfers between devices, body(): lax.all_to_all(proj_out, 'head', split_axis=1, concat_axis=0, tiled=True)  3.48 us
  transfers between devices with their start and end apart: 6, of which 6 were waited for; matrix products, arithmetic and copies ran while one was open for 4% of the time, Pallas kernels for 0%

profile of v1, /device:TPU:0, one launch (start us, length us, event | category | flops | bytes accessed | tf_op | source)
XLA Modules:
  0.0 111.6 jit_solution(17071096278130840655)
XLA Ops:
  6.5 0.0 copy-start
  6.5 0.0 copy-start.1
  6.5 1.1 %slice_bitcast_fusion = (bf16[2,1,128,256]{3,2,1,0:T(8,128)(2,1)S(1)}, bf16[2,128,256]{2,1,0:T(8,128)(2,1)S(1)}) fusion(bf16[4,128,256]{2,1,0:T(8,128)(2,1)} %param.4), kind=kLoop, calls=%fused_computation.23 | loop fusion | bytes 524288 | tf_op jit(solution)/shard_map/stack | solution.py:27
  7.7 0.7 pad_maximum_fusion
  8.4 4.3 %all-to-all-start = ((bf16[4,128,256]{2,1,0:T(8,128)(2,1)}), bf16[4,128,256]{2,1,0:T(8,128)(2,1)S(1)}, u32[]{:S(2)}, u32[]{:S(2)}) async-start(bf16[4,128,256]{2,1,0:T(8,128)(2,1)} %bitcast.2), calls=%async_computation | async-start | bytes 524288 | tf_op jit(solution)/shard_map/all_to_all | solution.py:29
  12.7 0.0 all-gather.2.cloned.1.call-start
  12.7 0.1 add_multiply_fusion
  12.8 5.8 %all-to-all-done = bf16[4,128,256]{2,1,0:T(8,128)(2,1)S(1)} async-done(((bf16[4,128,256]{2,1,0:T(8,128)(2,1)}), bf16[4,128,256]{2,1,0:T(8,128)(2,1)S(1)}, u32[]{:S(2)}, u32[]{:S(2)}) %all-to-all-start) | async-done | bytes 262176 | tf_op jit(solution)/shard_map/all_to_all | solution.py:29
  18.6 1.8 %collective-permute-start = (bf16[2,256,256]{2,1,0:T(8,128)(2,1)S(1)}, bf16[2,256,256]{2,1,0:T(8,128)(2,1)S(1)}, u32[]{:S(2)}, u32[]{:S(2)}) collective-permute-start(bf16[2,256,256]{2,1,0:T(8,128)(2,1)S(1)} %bitcast.53), channel_id=1, source_target_pairs={{0,1},{1,2},{2,3},{3,0},{4,5},{5,6},{6,7},{7,4},{8,9},{9,10},{10,1... | collective-permute-start | bytes 786440 | tf_op jit(solution)/shard_map/ppermute | solution.py:32
  20.4 0.1 add_bitcast_fusion.1
  20.5 7.4 %collective-permute-done = bf16[2,256,256]{2,1,0:T(8,128)(2,1)S(1)} collective-permute-done((bf16[2,256,256]{2,1,0:T(8,128)(2,1)S(1)}, bf16[2,256,256]{2,1,0:T(8,128)(2,1)S(1)}, u32[]{:S(2)}, u32[]{:S(2)}) %collective-permute-start) | collective-permute-done | bytes 262176 | tf_op jit(solution)/shard_map/ppermute | solution.py:32
  27.9 0.0 collective-permute-start.1
  27.9 0.1 add_bitcast_fusion
  28.0 0.0 copy-done.1
  28.0 0.2 reduce-window.8
  28.2 0.1 convert_reduce_fusion.1
  28.3 8.1 %collective-permute-done.1 = bf16[2,256,256]{2,1,0:T(8,128)(2,1)S(1)} collective-permute-done((bf16[2,256,256]{2,1,0:T(8,128)(2,1)S(1)}, bf16[2,256,256]{2,1,0:T(8,128)(2,1)S(1)}, u32[]{:S(2)}, u32[]{:S(2)}) %collective-permute-start.1) | collective-permute-done | bytes 262176 | tf_op jit(solution)/shard_map/ppermute | solution.py:32
  36.3 0.0 collective-permute-start.2
  36.3 0.1 convert_reduce_fusion.2
  36.4 1.3 %compare_and_fusion = pred[512,1024]{1,0:T(8,128)(4,1)} fusion(s32[1024]{0:T(1024)S(1)} %bitcast.64, s32[1024]{0:T(1024)S(1)} %convert_reduce_fusion.1, s32[512]{0:T(512)S(1)} %bitcast.66, s32[512]{0:T(512)S(1)} %convert_reduce_fusion.2), kind=kLoop, calls=%fused_computation.8 | loop fusion | flops 1572864 | bytes 536576 | tf_op jit(solution)/shard_map/while/body/eval_jaxpr/and | solution.py:82
  37.7 6.8 %collective-permute-done.2 = bf16[2,256,256]{2,1,0:T(8,128)(2,1)S(1)} collective-permute-done((bf16[2,256,256]{2,1,0:T(8,128)(2,1)S(1)}, bf16[2,256,256]{2,1,0:T(8,128)(2,1)S(1)}, u32[]{:S(2)}, u32[]{:S(2)}) %collective-permute-start.2) | collective-permute-done | bytes 262176 | tf_op jit(solution)/shard_map/ppermute | solution.py:32
  44.8 0.2 convert_reduce_fusion
  45.0 0.4 multiply_reduce_fusion
  45.5 0.3 fusion.1
  45.8 0.0 copy-done
  45.8 1.5 %multiply_convert_fusion = bf16[512,4,256]{2,0,1:T(8,128)(2,1)S(1)} fusion(bf16[1024,4,256]{2,1,0:T(4,128)(2,1)S(1)} %copy-done, bf16[512,1024]{1,0:T(8,128)(2,1)S(1)} %fusion.1), kind=kOutput, calls=%fused_computation.6 | convolution fusion | flops 1076363264 | bytes 4194304 | tf_op jit(solution)/shard_map/rd,dgc->rgc/dot_general | solution.py:50
  47.3 0.9 fusion.22
  48.2 7.6 %all_gather.10 = bf16[4,256,256]{2,1,0:T(8,128)(2,1)S(1)} all-gather(bf16[2,256,256]{2,1,0:T(8,128)(2,1)S(1)} %bitcast.59), channel_id=1, replica_groups=mesh['dp'=4,'ctx'=2,'head'=4] {'ctx'}, dimensions={0}, use_global_device_ids=true | all-gather | bytes 786432 | tf_op jit(solution)/shard_map/all_gather | solution.py:70
  55.8 0.9 reshape.244
  56.7 7.0 %all_gather.9 = bf16[4,256,256]{2,1,0:T(8,128)(2,1)S(1)} all-gather(bf16[2,256,256]{2,1,0:T(8,128)(2,1)S(1)} %bitcast.58), channel_id=1, replica_groups=mesh['dp'=4,'ctx'=2,'head'=4] {'ctx'}, dimensions={0}, use_global_device_ids=true | all-gather | bytes 786432 | tf_op jit(solution)/shard_map/all_gather | solution.py:71
  63.7 0.9 reshape.251
  64.7 0.1 reshape_squeeze.11
  64.7 3.5 %fusion.23 = (f32[512,2]{0,1:T(2,128)S(1)}, f32[512,2,128]{0,2,1:T(8,128)S(1)}) fusion(pred[512,1024]{1,0:T(8,128)(4,1)} %compare_and_fusion, bf16[1024,2,128]{2,1,0:T(2,128)(2,1)} %reshape.244, bf16[512,2,128]{2,1,0:T(2,128)(2,1)S(1)} %reshape_squeeze.11, bf16[1024,2,128]{2,1,0:T(2,128)(2,1)} %reshape.251), kind=kOutput, calls=%fused_computation.53 | convolution fusion | flops 544340992 | bytes 2363392 | tf_op jit(solution)/shard_map/while/body/eval_jaxpr/hqk,khd->qhd/dot_general | solution.py:91
  68.3 0.1 multiply_reduce_fusion.1
  68.4 1.2 %copy.43 = f32[512,1,256]{0,2,1:T(8,128)S(1)} copy(f32[512,1,256]{2,0,1:T(8,128)} %get-tuple-element.24) | data formatting | bytes 1048576 | tf_op jit(solution)/shard_map/convert_element_type | solution.py:96
  69.6 0.8 multiply_convert_fusion.1
  70.5 0.0 all-gather.2.cloned.1.call-update
  70.5 2.1 %copy.40 = bf16[256,1024]{0,1:T(8,128)(2,1)} copy(bf16[256,1024]{1,0:T(8,128)(2,1)} %param.7) | data formatting | bytes 1048576 | tf_op args[3]
  72.5 3.5 %all-to-all-start.1 = ((bf16[256,4,256]{0,2,1:T(8,128)(2,1)}), bf16[256,4,256]{0,2,1:T(8,128)(2,1)S(1)}, u32[]{:S(2)}, u32[]{:S(2)}) async-start(bf16[256,4,256]{0,2,1:T(8,128)(2,1)} %bitcast.19), calls=%async_computation.1 | async-start | bytes 1048576 | tf_op jit(solution)/shard_map/all_to_all | solution.py:100
  76.1 23.0 %all-to-all-done.1 = bf16[256,4,256]{0,2,1:T(8,128)(2,1)S(1)} async-done(((bf16[256,4,256]{0,2,1:T(8,128)(2,1)}), bf16[256,4,256]{0,2,1:T(8,128)(2,1)S(1)}, u32[]{:S(2)}, u32[]{:S(2)}) %all-to-all-start.1) | async-done | bytes 524320 | tf_op jit(solution)/shard_map/all_to_all | solution.py:100
  99.1 1.0 copy.41
  100.1 2.1 %all-gather.2.cloned.1.call-done = bf16[512,1024]{0,1:T(8,128)(2,1)} async-done(((bf16[512,256]{0,1:T(8,128)(2,1)}), bf16[512,1024]{0,1:T(8,128)(2,1)}) %all-gather.2.cloned.1.call-update) | async-done | bytes 1048592 | tf_op jit(solution)/shard_map/all_gather | solution.py:102
  102.2 2.5 %fusion.6 = bf16[512,256]{1,0:T(8,128)(2,1)} fusion(f32[512,256]{1,0:T(8,128)S(1)} %bitcast.61, bf16[512,1024]{0,1:T(8,128)(2,1)} %all-gather.2.cloned.1.call-done, bf16[1024,256]{1,0:T(8,128)(2,1)} %bitcast.62), kind=kOutput, calls=%fused_computation.12 | convolution fusion | flops 268697600 | bytes 2359296 | tf_op jit(solution)/shard_map/dot_general | solution.py:101
  (20 shorter events, 0.3 us)
Async XLA Ops:
  6.5 39.2 %copy-start = (bf16[1024,4,256]{2,1,0:T(4,128)(2,1)S(1)}, bf16[1024,4,256]{2,1,0:T(4,128)(2,1)}, u32[]{:S(2)}) copy-start(bf16[1024,4,256]{2,1,0:T(4,128)(2,1)} %param.6) | copy-start | bytes 6291460
  6.5 21.5 %copy-start.1 = (s32[4]{0:T(128)S(1)}, s32[4]{0:T(128)}, u32[]{:S(2)}) copy-start(s32[4]{0:T(128)} %param.5) | copy-start | bytes 52
  8.4 10.1 %all-to-all-start = ((bf16[4,128,256]{2,1,0:T(8,128)(2,1)}), bf16[4,128,256]{2,1,0:T(8,128)(2,1)S(1)}, u32[]{:S(2)}, u32[]{:S(2)}) async-start(bf16[4,128,256]{2,1,0:T(8,128)(2,1)} %bitcast.2), calls=%async_computation | async-start | bytes 524288 | tf_op jit(solution)/shard_map/all_to_all | solution.py:29
  12.7 89.5 %all-gather.2.cloned.1.call-start = ((), (), s32[]{:S(2)}) async-start(), calls=%async_computation.2 | async-start | bytes 1310720 | tf_op jit(solution)/shard_map/all_gather | solution.py:102
  18.6 9.3 %collective-permute-start = (bf16[2,256,256]{2,1,0:T(8,128)(2,1)S(1)}, bf16[2,256,256]{2,1,0:T(8,128)(2,1)S(1)}, u32[]{:S(2)}, u32[]{:S(2)}) collective-permute-start(bf16[2,256,256]{2,1,0:T(8,128)(2,1)S(1)} %bitcast.53), channel_id=1, source_target_pairs={{0,1},{1,2},{2,3},{3,0},{4,5},{5,6},{6,7},{7,4},{8,9},{9,10},{10,1... | collective-permute-start | bytes 786440 | tf_op jit(solution)/shard_map/ppermute | solution.py:32
  27.9 8.4 %collective-permute-start.1 = (bf16[2,256,256]{2,1,0:T(8,128)(2,1)S(1)}, bf16[2,256,256]{2,1,0:T(8,128)(2,1)S(1)}, u32[]{:S(2)}, u32[]{:S(2)}) collective-permute-start(bf16[2,256,256]{2,1,0:T(8,128)(2,1)S(1)} %collective-permute-done), channel_id=1, source_target_pairs={{0,1},{1,2},{2,3},{3,0},{4,5},{5,6},{6,7},{7,4},{8,9},{9,10},{10,1... | collective-permute-start | bytes 786440 | tf_op jit(solution)/shard_map/ppermute | solution.py:32
  36.3 8.2 %collective-permute-start.2 = (bf16[2,256,256]{2,1,0:T(8,128)(2,1)S(1)}, bf16[2,256,256]{2,1,0:T(8,128)(2,1)S(1)}, u32[]{:S(2)}, u32[]{:S(2)}) collective-permute-start(bf16[2,256,256]{2,1,0:T(8,128)(2,1)S(1)} %collective-permute-done.1), channel_id=1, source_target_pairs={{0,1},{1,2},{2,3},{3,0},{4,5},{5,6},{6,7},{7,4},{8,9},{9,10},{10,1... | collective-permute-start | bytes 786440 | tf_op jit(solution)/shard_map/ppermute | solution.py:32
  72.5 26.5 %all-to-all-start.1 = ((bf16[256,4,256]{0,2,1:T(8,128)(2,1)}), bf16[256,4,256]{0,2,1:T(8,128)(2,1)S(1)}, u32[]{:S(2)}, u32[]{:S(2)}) async-start(bf16[256,4,256]{0,2,1:T(8,128)(2,1)} %bitcast.19), calls=%async_computation.1 | async-start | bytes 1048576 | tf_op jit(solution)/shard_map/all_to_all | solution.py:100
Sparse Core Ops, SparseCore 0:
  70.6 31.5 all-gather.1
